TPU v7x, 32 devices: a whole 2x2x4 slice. The times are simulated.
32 devices in a mesh: rep: 2 (over core), grp: 16 (over z, y, x).
Axes of the slice: x: 2, y: 2, z: 4, core: 2. Of those that a mesh axis runs over, the one named last changes fastest.
Arguments:
- grad_parts: float32 [2, 1024, 9216], P('rep', 'grp'), may hold values from -6 to 6
- gain_grad_parts: float32 [2, 2, 1024], P('rep', None, 'grp'), may hold values from -6 to 6
- weights: float32 [1024, 9216], P('grp'), may hold values from -0.1875 to 0.1875
- basis: float32 [1024, 256], P('grp'), may hold values from -0.1875 to 0.1875
- moment_first: float32 [9216, 256], P('grp'), may hold values from -12 to 12
- moment_second: float32 [9216, 256], P('grp'), may hold values from 0.01 to 1
- gains: float32 [2, 1024], P(None, 'grp'), may hold values from 0.5 to 1.5
- gain_first: float32 [2, 1024], P(None, 'grp'), may hold values from -12 to 12
- gain_second: float32 [2, 1024], P(None, 'grp'), may hold values from 0.01 to 1
Outputs:
- new_weights: float32 [1024, 9216], P('grp')
- new_first: float32 [9216, 256], P('grp')
- new_second: float32 [9216, 256], P('grp')
- new_basis: float32 [1024, 256], P('grp')
- new_gains: float32 [2, 1024], P(None, 'grp')
- new_gain_first: float32 [2, 1024], P(None, 'grp')
- new_gain_second: float32 [2, 1024], P(None, 'grp')
All inputs are finite; a program needn't handle non-finite values.
Results may differ from a plain program's by a relative error of at most 0.0001.
Values sent between devices are 32-bit elements; how exact they have to be, the bound alone decides.
A program may use at most 64 MiB of HBM per device.

v0:
```python
import jax
import jax.numpy as jnp
from jax import lax
from jax.sharding import PartitionSpec as P

NS_STEPS = 3
beta_first = 0.9
beta_second = 0.999
learn_rate = 0.1
galore_scale = 0.25
adam_eps = 1e-08


def exact_dot(left, right):
    return jnp.dot(left, right, precision=lax.Precision.HIGHEST, preferred_element_type=jnp.float32)


def body(
    grad_parts,
    gain_grad_parts,
    weights,
    basis,
    moment_first,
    moment_second,
    gains,
    gain_first,
    gain_second,
):
    corr_first = 1.0 - beta_first**10
    corr_second = 1.0 - beta_second**10
    local_grad = grad_parts[0]
    local_gain = gain_grad_parts[0]
    source, gain_grad = lax.psum((local_grad, local_gain), "rep")
    col_block = lax.all_to_all(source, "grp", split_axis=1, concat_axis=0, tiled=True)
    full_basis = lax.all_gather(basis, "grp", axis=0, tiled=True)
    projected = exact_dot(col_block.T, full_basis)
    new_first = beta_first * moment_first + (1.0 - beta_first) * projected
    new_second = beta_second * moment_second + (1.0 - beta_second) * projected * projected
    direction = new_first / corr_first / (jnp.sqrt(new_second / corr_second) + adam_eps)
    subspace = lax.psum_scatter(
        exact_dot(col_block, projected), "grp", scatter_dimension=0, tiled=True
    )
    update_cols = exact_dot(full_basis, direction.T)
    update = lax.all_to_all(update_cols, "grp", split_axis=0, concat_axis=1, tiled=True)
    new_weights = weights - learn_rate * galore_scale * update
    gram = lax.psum(exact_dot(subspace.T, subspace), "grp")
    scale = jnp.sqrt(jnp.sqrt(jnp.sum(gram * gram) + 1e-06))
    iterate = subspace / scale
    current = lax.psum(exact_dot(iterate.T, iterate), "grp")
    for step in range(NS_STEPS):
        iterate = 1.5 * iterate - 0.5 * exact_dot(iterate, current)
        if step + 1 < NS_STEPS:
            current = lax.psum(exact_dot(iterate.T, iterate), "grp")
    new_gain_first = beta_first * gain_first + (1.0 - beta_first) * gain_grad
    new_gain_second = beta_second * gain_second + (1.0 - beta_second) * gain_grad * gain_grad
    new_gains = gains - learn_rate * (new_gain_first / corr_first) / (
        jnp.sqrt(new_gain_second / corr_second) + adam_eps
    )
    return (new_weights, new_first, new_second, iterate, new_gains, new_gain_first, new_gain_second)


def solution(mesh):
    in_specs = (
        P("rep", "grp", None),
        P("rep", None, "grp"),
        P("grp", None),
        P("grp", None),
        P("grp", None),
        P("grp", None),
        P(None, "grp"),
        P(None, "grp"),
        P(None, "grp"),
    )
    out_specs = (
        P("grp", None),
        P("grp", None),
        P("grp", None),
        P("grp", None),
        P(None, "grp"),
        P(None, "grp"),
        P(None, "grp"),
    )
    return jax.shard_map(body, mesh=mesh, in_specs=in_specs, out_specs=out_specs, check_vma=False)
```

profile of v0, /device:TPU:0, one launch (start us, length us, event | category | flops | bytes accessed | tf_op | source)
XLA Modules:
  0.0 698.1 jit_solution(16123633923945637209)
XLA Ops:
  8.0 2.2 all_to_all.24
  10.2 2.3 copy.34
  12.6 25.1 %all-reduce.6.cloned.1.call-done = f32[64,16,576]{2,0,1:T(8,128)} async-done(((f32[64,16,576]{2,0,1:T(8,128)}), f32[64,16,576]{2,0,1:T(8,128)}) %all-reduce.6.cloned.1.call-update) | async-done | bytes 2359312 | tf_op jit(solution)/shard_map/psum | solution.py:33
  37.7 6.8 all-to-all-start
  44.6 0.5 all-gather.2.cloned.1.call-update
  45.1 83.0 %all-gather.2.cloned.1.call-done = f32[1024,256]{1,0:T(8,128)} async-done(((f32[64,256]{1,0:T(8,128)}), f32[1024,256]{1,0:T(8,128)}) %all-gather.2.cloned.1.call-update) | async-done | bytes 1048592 | tf_op jit(solution)/shard_map/all_gather | solution.py:35
  128.1 6.7 multiply_add_fusion
  134.8 5.5 convolution_bitcast_fusion.1
  140.3 2.6 copy.38
  142.9 3.8 convolution_bitcast_fusion
  146.7 2.1 copy.35
  148.8 4.5 all-to-all-start.1
  153.4 80.3 %reduce-scatter.4.cloned.1.call-done = f32[64,256]{1,0:T(8,128)} async-done(((f32[1024,256]{1,0:T(8,128)}), f32[64,256]{1,0:T(8,128)}) %reduce-scatter.4.cloned.1.call-update) | async-done | bytes 65552
  233.7 2.0 fusion.18
  235.8 0.2 all-reduce.10.cloned.1.call-start
  236.0 109.0 %all-reduce.8.cloned.1.call-done = f32[256,256]{1,0:T(8,128)} async-done(((f32[256,256]{1,0:T(8,128)}), f32[256,256]{1,0:T(8,128)}) %all-reduce.8.cloned.1.call-update) | async-done | bytes 262160 | tf_op jit(solution)/shard_map/psum | solution.py:46
  345.0 1.6 multiply_reduce_fusion
  347.4 2.0 fusion.12
  349.5 107.5 %all-reduce.10.cloned.1.call-done = f32[256,256]{1,0:T(8,128)} async-done(((f32[256,256]{1,0:T(8,128)}), f32[256,256]{1,0:T(8,128)}) %all-reduce.10.cloned.1.call-update) | async-done | bytes 262160 | tf_op jit(solution)/shard_map/psum | solution.py:49
  457.0 1.2 fusion.2
  458.2 1.1 fusion.19
  459.4 109.6 %all-reduce.12.cloned.1.call-done = f32[256,256]{1,0:T(8,128)} async-done(((f32[256,256]{1,0:T(8,128)}), f32[256,256]{1,0:T(8,128)}) %all-reduce.12.cloned.1.call-update) | async-done | bytes 262160 | tf_op jit(solution)/shard_map/psum | solution.py:53
  569.0 1.2 fusion.1
  570.2 1.1 fusion.20
  571.4 2.5 psum.47
  573.8 0.6 divide_subtract_fusion
  574.4 106.6 %all-reduce.14.cloned.1.call-done = f32[256,256]{1,0:T(8,128)} async-done(((f32[256,256]{1,0:T(8,128)}), f32[256,256]{1,0:T(8,128)}) %all-reduce.14.cloned.1.call-update) | async-done | bytes 262160 | tf_op jit(solution)/shard_map/psum | solution.py:53
  681.0 1.8 fusion
  682.8 0.2 multiply_bitcast_fusion
  683.1 1.5 copy.36
  684.6 2.0 mul.101
  686.6 4.0 sub.15
  (24 shorter events, 0.4 us)
Async XLA Ops:
  8.0 29.7 %all-reduce.6.cloned.1.call-start = ((), (), s32[]{:S(2)}) async-start(), calls=%async_computation.3 | async-start | bytes 5242880 | tf_op jit(solution)/shard_map/psum | solution.py:33
  37.7 90.4 %all-to-all-start = ((f32[64,16,576]{2,0,1:T(8,128)}), f32[64,16,576]{2,0,1:T(8,128)S(1)}, u32[]{:S(2)}, u32[]{:S(2)}) async-start(f32[64,16,576]{2,0,1:T(8,128)} %all-reduce.6.cloned.1.call-done), calls=%async_computation | async-start | bytes 5242880 | tf_op jit(solution)/shard_map/all_to_all | solution.py:34
  44.5 83.6 %all-gather.2.cloned.1.call-start = ((), (), s32[]{:S(2)}) async-start(), calls=%async_computation.4 | async-start | bytes 1114112 | tf_op jit(solution)/shard_map/all_gather | solution.py:35
  45.1 188.7 %reduce-scatter.4.cloned.1.call-start = ((), (), s32[]{:S(2)}) async-start(), calls=%async_computation.9 | async-start | bytes 1114112
  134.8 8.1 %copy-start = (f32[576,256]{1,0:T(8,128)}, f32[576,256]{1,0:T(8,128)S(1)}, u32[]{:S(2)}) copy-start(f32[576,256]{1,0:T(8,128)S(1)} %get-tuple-element.31) | copy-start | bytes 1769476
  148.8 534.0 %all-to-all-start.1 = ((f32[16,64,576]{2,1,0:T(8,128)}), f32[16,64,576]{2,1,0:T(8,128)S(1)}, u32[]{:S(2)}, u32[]{:S(2)}) async-start(f32[16,64,576]{2,1,0:T(8,128)} %bitcast.30), calls=%async_computation.1 | async-start | bytes 5242880 | tf_op jit(solution)/shard_map/all_to_all | solution.py:44
  153.3 418.1 %copy-start.4 = (f32[1,2,64]{2,1,0:T(2,128)S(1)}, f32[1,2,64]{2,1,0:T(2,128)}, u32[]{:S(2)}) copy-start(f32[1,2,64]{2,1,0:T(2,128)} %param.10) | copy-start | bytes 1540
  153.3 420.5 %copy-start.1 = (f32[2,64]{1,0:T(2,128)S(1)}, f32[2,64]{1,0:T(2,128)}, u32[]{:S(2)}) copy-start(f32[2,64]{1,0:T(2,128)} %param.15) | copy-start | bytes 1540
  153.3 420.5 %copy-start.2 = (f32[2,64]{1,0:T(2,128)S(1)}, f32[2,64]{1,0:T(2,128)}, u32[]{:S(2)}) copy-start(f32[2,64]{1,0:T(2,128)} %param.16) | copy-start | bytes 1540
  153.3 420.5 %copy-start.3 = (f32[2,64]{1,0:T(2,128)S(1)}, f32[2,64]{1,0:T(2,128)}, u32[]{:S(2)}) copy-start(f32[2,64]{1,0:T(2,128)} %param.17) | copy-start | bytes 1540
  153.3 191.7 %all-reduce.8.cloned.1.call-start = ((), (), s32[]{:S(2)}) async-start(), calls=%async_computation.5 | async-start | bytes 524288 | tf_op jit(solution)/shard_map/psum | solution.py:46
  235.8 221.2 %all-reduce.10.cloned.1.call-start = ((), (), s32[]{:S(2)}) async-start(), calls=%async_computation.6 | async-start | bytes 524288 | tf_op jit(solution)/shard_map/psum | solution.py:49
  349.5 219.5 %all-reduce.12.cloned.1.call-start = ((), (), s32[]{:S(2)}) async-start(), calls=%async_computation.7 | async-start | bytes 524288 | tf_op jit(solution)/shard_map/psum | solution.py:53
  459.4 221.6 %all-reduce.14.cloned.1.call-start = ((), (), s32[]{:S(2)}) async-start(), calls=%async_computation.8 | async-start | bytes 524288 | tf_op jit(solution)/shard_map/psum | solution.py:53
Sparse Core Ops, SparseCore 0:
  12.7 24.9 all-reduce.5
Sparse Core Ops, SparseCore 1:
  47.8 80.3 all-gather.1
  143.0 90.7 reduce-scatter.3
  239.4 105.6 all-reduce.7
  350.9 106.1 all-reduce.9
  462.8 106.1 all-reduce.11
  574.8 106.1 all-reduce.13
where the time goes:
time: 699 us; the launch traced here: 698 us
  waiting for transfers between devices  622 us (89%)
  matrix products  26.5 us (4%)
  between operations  16.4 us (2%)
  local copies, waits for them, and re-layouts  12.7 us (2%)
  starting transfers between devices  11.8 us (2%)
    psum x3, waiting for transfers between devices, body(): current = lax.psum(exact_dot(iterate.T, iterate), 'grp')  324 us
    psum x1, waiting for transfers between devices, body(): gram = lax.psum(exact_dot(subspace.T, subspace), 'grp')  109 us
    all_gather x1, waiting for transfers between devices, body(): full_basis = lax.all_gather(basis, 'grp', axis=0, tiled=True)  83 us
    unnamed x8, waiting for transfers between devices  81 us
    dot_general x10, matrix products, exact_dot(): jnp.dot(left, right, precision=lax.Precision.HIGHEST, preferred_element_t...  26.5 us
    psum x1, waiting for transfers between devices, body(): source, gain_grad = lax.psum((local_grad, local_gain), 'rep')  25.1 us
  transfers between devices with their start and end apart: 9, of which 7 were waited for; matrix products, arithmetic and copies ran while one was open for 3% of the time, Pallas kernels for 0%

commit v1 on v0

--- a/solution.py
+++ b/solution.py
@@ -43,7 +43,8 @@
     update_cols = exact_dot(full_basis, direction.T)
     update = lax.all_to_all(update_cols, "grp", split_axis=0, concat_axis=1, tiled=True)
     new_weights = weights - learn_rate * galore_scale * update
-    gram = lax.psum(exact_dot(subspace.T, subspace), "grp")
+    thing_lift = lambda payload: lax.all_gather(payload, "grp").sum(axis=0)
+    gram = thing_lift(exact_dot(subspace.T, subspace))
     scale = jnp.sqrt(jnp.sqrt(jnp.sum(gram * gram) + 1e-06))
     iterate = subspace / scale
     current = lax.psum(exact_dot(iterate.T, iterate), "grp")

time: 699 us -> 669 us (0.957)
  waiting for transfers between devices: 622 us -> 592 us
    psum x1 -> x0, waiting for transfers between devices: 109 us -> none  [body(): gram = lax.psum(exact_dot(subspace.T, subspace), 'grp')]
    all_gather x0 -> x1, waiting for transfers between devices: none -> 90.9 us  [body(): thing_lift = lambda payload: lax.all_gather(payload, 'grp').sum(axis=0)]
    psum x3, waiting for transfers between devices: 324 us -> 315 us  [body(): current = lax.psum(exact_dot(iterate.T, iterate), 'grp')]
where the time goes in v1:
time: 669 us; the launch traced here: 668 us
  waiting for transfers between devices  592 us (88%)
  matrix products  25.4 us (4%)
  between operations  16.4 us (2%)
  local copies, waits for them, and re-layouts  12.8 us (2%)
  starting transfers between devices  11 us (2%)
  other arithmetic  8.02 us (1%)
    psum x3, waiting for transfers between devices, body(): current = lax.psum(exact_dot(iterate.T, iterate), 'grp')  315 us
    all_gather x1, waiting for transfers between devices, body(): thing_lift = lambda payload: lax.all_gather(payload, 'grp').sum(axis=0)  90.9 us
    all_gather x1, waiting for transfers between devices, body(): full_basis = lax.all_gather(basis, 'grp', axis=0, tiled=True)  83 us
    unnamed x8, waiting for transfers between devices  78.2 us
    dot_general x10, matrix products, exact_dot(): jnp.dot(left, right, precision=lax.Precision.HIGHEST, preferred_element_t...  25.4 us
    psum x1, waiting for transfers between devices, body(): source, gain_grad = lax.psum((local_grad, local_gain), 'rep')  25.1 us
  transfers between devices with their start and end apart: 9, of which 7 were waited for; matrix products, arithmetic and copies ran while one was open for 3% of the time, Pallas kernels for 0%

profile of v1, /device:TPU:0, one launch (start us, length us, event | category | flops | bytes accessed | tf_op | source)
XLA Modules:
  0.0 668.0 jit_solution(6917661218397143144)
XLA Ops:
  8.0 2.2 all_to_all.24
  10.2 2.3 copy.38
  12.6 25.1 %all-reduce.5.cloned.1.call-done = f32[64,16,576]{2,0,1:T(8,128)} async-done(((f32[64,16,576]{2,0,1:T(8,128)}), f32[64,16,576]{2,0,1:T(8,128)}) %all-reduce.5.cloned.1.call-update) | async-done | bytes 2359312 | tf_op jit(solution)/shard_map/psum | solution.py:33
  37.7 6.8 %all-to-all-start = ((f32[64,16,576]{2,0,1:T(8,128)}), f32[64,16,576]{2,0,1:T(8,128)S(1)}, u32[]{:S(2)}, u32[]{:S(2)}) async-start(f32[64,16,576]{2,0,1:T(8,128)} %all-reduce.5.cloned.1.call-done), calls=%async_computation | async-start | bytes 5242880 | tf_op jit(solution)/shard_map/all_to_all | solution.py:34
  44.6 0.5 all-gather.4.cloned.1.call-update
  45.1 83.0 %all-gather.4.cloned.1.call-done = f32[1024,256]{1,0:T(8,128)} async-done(((f32[64,256]{1,0:T(8,128)}), f32[1024,256]{1,0:T(8,128)}) %all-gather.4.cloned.1.call-update) | async-done | bytes 1048592 | tf_op jit(solution)/shard_map/all_gather | solution.py:35
  128.1 6.7 %multiply_add_fusion = (f32[576,256]{1,0:T(8,128)}, f32[576,256]{1,0:T(8,128)}, f32[576,256]{1,0:T(8,128)S(1)}) fusion(f32[576,256]{1,0:T(8,128)S(1)} %copy-done.1, f32[576,256]{1,0:T(8,128)} %param.14, f32[1024,576]{1,0:T(8,128)S(1)} %bitcast.29, f32[1024,256]{1,0:T(8,128)} %all-gather.4.cloned.1.call-done), kind=kOutput, calls=%fused_computation.16 | convolution fusion | flops 1812971520 | bytes 6356992 | tf_op jit(solution)/shard_map/dot_general | solution.py:15
  134.8 5.5 convolution_bitcast_fusion.1
  140.4 2.6 copy.42
  143.2 77.6 %reduce-scatter.4.cloned.1.call-done = f32[64,256]{1,0:T(8,128)} async-done(((f32[1024,256]{1,0:T(8,128)}), f32[64,256]{1,0:T(8,128)}) %reduce-scatter.4.cloned.1.call-update) | async-done | bytes 65552
  220.8 2.0 fusion.18
  222.9 3.6 convolution_bitcast_fusion
  226.5 2.1 copy.39
  228.6 3.7 all-to-all-start.1
  232.4 90.9 %all-gather.6.cloned.1.call-done = f32[4096,256]{1,0:T(8,128)} async-done(((f32[256,256]{1,0:T(8,128)}), f32[4096,256]{1,0:T(8,128)}) %all-gather.6.cloned.1.call-update) | async-done | bytes 4194320 | tf_op jit(solution)/shard_map/all_gather | solution.py:46
  323.3 2.5 reduce_sum.18
  325.8 0.7 multiply_reduce_fusion
  327.2 1.1 fusion.12
  328.5 106.9 %all-reduce.7.cloned.1.call-done = f32[256,256]{1,0:T(8,128)} async-done(((f32[256,256]{1,0:T(8,128)}), f32[256,256]{1,0:T(8,128)}) %all-reduce.7.cloned.1.call-update) | async-done | bytes 262160 | tf_op jit(solution)/shard_map/psum | solution.py:50
  435.3 1.2 fusion.2
  436.5 1.1 fusion.19
  437.7 2.5 psum.39
  440.2 0.6 divide_subtract_fusion
  440.8 106.5 %all-reduce.9.cloned.1.call-done = f32[256,256]{1,0:T(8,128)} async-done(((f32[256,256]{1,0:T(8,128)}), f32[256,256]{1,0:T(8,128)}) %all-reduce.9.cloned.1.call-update) | async-done | bytes 262160 | tf_op jit(solution)/shard_map/psum | solution.py:54
  547.3 1.2 fusion.1
  548.5 1.1 fusion.20
  549.7 0.2 multiply_bitcast_fusion
  549.9 1.5 copy.40
  551.4 2.0 mul.101
  553.5 4.0 sub.15
  557.5 101.2 %all-reduce.11.cloned.1.call-done = f32[256,256]{1,0:T(8,128)} async-done(((f32[256,256]{1,0:T(8,128)}), f32[256,256]{1,0:T(8,128)}) %all-reduce.11.cloned.1.call-update) | async-done | bytes 262160 | tf_op jit(solution)/shard_map/psum | solution.py:54
  658.7 1.8 fusion
  (29 shorter events, 0.6 us)
Async XLA Ops:
  8.0 29.7 %all-reduce.5.cloned.1.call-start = ((), (), s32[]{:S(2)}) async-start(), calls=%async_computation.3 | async-start | bytes 5242880 | tf_op jit(solution)/shard_map/psum | solution.py:33
  12.6 115.6 %copy-start.1 = (f32[576,256]{1,0:T(8,128)S(1)}, f32[576,256]{1,0:T(8,128)}, u32[]{:S(2)}) copy-start(f32[576,256]{1,0:T(8,128)} %param.13) | copy-start | bytes 1769476
  37.7 90.4 %all-to-all-start = ((f32[64,16,576]{2,0,1:T(8,128)}), f32[64,16,576]{2,0,1:T(8,128)S(1)}, u32[]{:S(2)}, u32[]{:S(2)}) async-start(f32[64,16,576]{2,0,1:T(8,128)} %all-reduce.5.cloned.1.call-done), calls=%async_computation | async-start | bytes 5242880 | tf_op jit(solution)/shard_map/all_to_all | solution.py:34
  44.5 83.6 %all-gather.4.cloned.1.call-start = ((), (), s32[]{:S(2)}) async-start(), calls=%async_computation.4 | async-start | bytes 1114112 | tf_op jit(solution)/shard_map/all_gather | solution.py:35
  45.1 175.7 %reduce-scatter.4.cloned.1.call-start = ((), (), s32[]{:S(2)}) async-start(), calls=%async_computation.9 | async-start | bytes 1114112
  140.4 82.5 %copy-start = (f32[1024,256]{1,0:T(8,128)S(1)}, f32[1024,256]{1,0:T(8,128)}, u32[]{:S(2)}) copy-start(f32[1024,256]{1,0:T(8,128)} %all-gather.4.cloned.1.call-done) | copy-start | bytes 3145732
  143.0 180.3 %all-gather.6.cloned.1.call-start = ((), (), s32[]{:S(2)}) async-start(), calls=%async_computation.8 | async-start | bytes 4456448 | tf_op jit(solution)/shard_map/all_gather | solution.py:46
  228.6 321.1 %all-to-all-start.1 = ((f32[16,64,576]{2,1,0:T(8,128)}), f32[16,64,576]{2,1,0:T(8,128)S(1)}, u32[]{:S(2)}, u32[]{:S(2)}) async-start(f32[16,64,576]{2,1,0:T(8,128)} %bitcast.31), calls=%async_computation.1 | async-start | bytes 5242880 | tf_op jit(solution)/shard_map/all_to_all | solution.py:44
  232.3 94.9 %copy-start.2 = (f32[64,256]{1,0:T(8,128)S(1)}, f32[64,256]{1,0:T(8,128)}, u32[]{:S(2)}) copy-start(f32[64,256]{1,0:T(8,128)} %reduce-scatter.4.cloned.1.call-done) | copy-start | bytes 196612
  232.3 203.0 %all-reduce.7.cloned.1.call-start = ((), (), s32[]{:S(2)}) async-start(), calls=%async_computation.5 | async-start | bytes 524288 | tf_op jit(solution)/shard_map/psum | solution.py:50
  323.3 114.4 %copy-start.6 = (f32[1,2,64]{2,1,0:T(2,128)S(1)}, f32[1,2,64]{2,1,0:T(2,128)}, u32[]{:S(2)}) copy-start(f32[1,2,64]{2,1,0:T(2,128)} %param.10) | copy-start | bytes 1540
  323.3 116.9 %copy-start.3 = (f32[2,64]{1,0:T(2,128)S(1)}, f32[2,64]{1,0:T(2,128)}, u32[]{:S(2)}) copy-start(f32[2,64]{1,0:T(2,128)} %param.15) | copy-start | bytes 1540
  323.3 116.9 %copy-start.4 = (f32[2,64]{1,0:T(2,128)S(1)}, f32[2,64]{1,0:T(2,128)}, u32[]{:S(2)}) copy-start(f32[2,64]{1,0:T(2,128)} %param.16) | copy-start | bytes 1540
  323.3 116.9 %copy-start.5 = (f32[2,64]{1,0:T(2,128)S(1)}, f32[2,64]{1,0:T(2,128)}, u32[]{:S(2)}) copy-start(f32[2,64]{1,0:T(2,128)} %param.17) | copy-start | bytes 1540
  328.4 218.9 %all-reduce.9.cloned.1.call-start = ((), (), s32[]{:S(2)}) async-start(), calls=%async_computation.6 | async-start | bytes 524288 | tf_op jit(solution)/shard_map/psum | solution.py:54
  437.7 221.0 %all-reduce.11.cloned.1.call-start = ((), (), s32[]{:S(2)}) async-start(), calls=%async_computation.7 | async-start | bytes 524288 | tf_op jit(solution)/shard_map/psum | solution.py:54
Sparse Core Ops, SparseCore 0:
  12.7 24.9 all-reduce.4
Sparse Core Ops, SparseCore 1:
  47.8 80.3 all-gather.3
  143.1 77.7 reduce-scatter.3
  224.0 99.2 all-gather.5
  329.1 106.1 all-reduce.6
  441.1 106.1 all-reduce.8
  552.5 106.1 all-reduce.10
